TPU v7x, 32 devices: a whole 2x2x4 slice. The times are simulated.
32 devices in a mesh: dp: 8 (over y, x, core), mp: 4 (over z).
Axes of the slice: x: 2, y: 2, z: 4, core: 2. Of those that a mesh axis runs over, the one named last changes fastest.
Arguments:
- hidden: bfloat16 [4096, 768], P('dp'), may hold values from -6 to 6
- memory: bfloat16 [32768, 768], P('dp', 'mp'), may hold values from -6 to 6
- out_grad: bfloat16 [4096, 768], P('dp'), may hold values from -6 to 6
- dec_starts: int32 [32, 4], P('dp'), may hold values from 0 to 127, as said below
- dec_length: int32 [32], P('dp'), may hold values from 96 to 128
- mem_starts: int32 [32, 4], P('dp'), may hold values from 0 to 1023, as said below
- mem_length: int32 [32], P('dp'), may hold values from 768 to 1024
- self_qkv: bfloat16 [3, 768, 768], P(None, None, 'mp'), may hold values from -0.25 to 0.25
- self_qv_bias: float32 [2, 768], P(None, 'mp'), may hold values from -3 to 3
- self_proj: bfloat16 [768, 768], P('mp'), may hold values from -0.3125 to 0.3125
- cross_query: bfloat16 [768, 768], P(None, 'mp'), may hold values from -0.25 to 0.25
- cross_kv: bfloat16 [2, 768, 768], P(None, None, 'mp'), may hold values from -0.25 to 0.25
- cross_qv_bias: float32 [2, 768], P(None, 'mp'), may hold values from -3 to 3
- cross_proj: bfloat16 [768, 768], P('mp'), may hold values from -0.875 to 0.875
- ffn_in: bfloat16 [768, 3072], P(None, 'mp'), may hold values from -0.21875 to 0.21875
- ffn_in_bias: float32 [3072], P('mp'), may hold values from -3 to 3
- ffn_out: bfloat16 [3072, 768], P('mp'), may hold values from -0.15625 to 0.15625
- out_biases: float32 [3, 768], replicated, may hold values from -3 to 3
- norm_gains: float32 [3, 768], replicated, may hold values from 0.25 to 1.75
- norm_biases: float32 [3, 768], replicated, may hold values from -2 to 2
Outputs:
- result: bfloat16 [4096, 768], P('dp')
- hidden_grad: float32 [4096, 768], P('dp')
- memory_grad: float32 [32768, 768], P('dp', 'mp')
- self_qkv_grad: float32 [3, 768, 768], P(None, None, 'mp')
- self_qv_bias_grad: float32 [2, 768], P(None, 'mp')
- self_proj_grad: float32 [768, 768], P('mp')
- cross_query_grad: float32 [768, 768], P(None, 'mp')
- cross_kv_grad: float32 [2, 768, 768], P(None, None, 'mp')
- cross_qv_bias_grad: float32 [2, 768], P(None, 'mp')
- cross_proj_grad: float32 [768, 768], P('mp')
- ffn_in_grad: float32 [768, 3072], P(None, 'mp')
- ffn_in_bias_grad: float32 [3072], P('mp')
- ffn_out_grad: float32 [3072, 768], P('mp')
- out_biases_grad: float32 [3, 768], replicated
- norm_gains_grad: float32 [3, 768], replicated
- norm_biases_grad: float32 [3, 768], replicated
Inputs may be any that keep to these rules, and one draw needn't show every extreme that they name: `dec_starts`: each packed row holds 4 pairs; its offsets start at 0, rise strictly and stay below the row's used slots, so every decoder segment holds at least one used slot; padded slots belong to the last pair. `mem_starts`: pair j's table is memory segment j of the same packed row; offsets start at 0, rise strictly and stay below the row's used slots, so every memory segment holds at least one used slot.
All inputs are finite; a program needn't handle non-finite values.
Results may differ from a plain program's by a relative error of at most 0.023.
Values may be sent and summed in bfloat16 or wider, within the bound.
No kernel may reach another device: no remote copies, remote signals or barrier semaphores. Data moves between devices by JAX's collectives and lax.ppermute only.
A program may use at most 128 MiB of HBM per device.

v0:
```python
import jax
import jax.numpy as jnp
from jax import lax
from jax.sharding import PartitionSpec as P

HD = 64
NEG_FILL = -1000000000.0
EPSILON = 1e-05


def layer_norm(values, gain_row, bias_row):
    average = jnp.mean(values, -1, keepdims=True)
    centered = values - average
    variance = jnp.mean(centered * centered, -1, keepdims=True)
    return centered * lax.rsqrt(variance + EPSILON) * gain_row + bias_row


def exact_gelu(values):
    return jax.nn.gelu(values, approximate=False)


def segment_ids(starts, slot_count):
    places = jnp.arange(slot_count, dtype=jnp.int32)
    return jnp.sum((starts[:, None, :] <= places[None, :, None]).astype(jnp.int32), -1) - 1


def inner_dot(left_side, right_side):
    return lax.dot_general(
        left_side, right_side, (((0,), (0,)), ((), ())), preferred_element_type=jnp.float32
    )


def outer_dot(left_side, right_side):
    return lax.dot_general(
        left_side, right_side, (((1,), (1,)), ((), ())), preferred_element_type=jnp.float32
    )


def row_groups(kernel, arrays):
    row_count = arrays[0].shape[0]
    limit = max(1, 512 // arrays[0].shape[1])
    group_rows = max(
        (count for count in range(1, min(row_count, limit) + 1) if row_count % count == 0)
    )
    blocks = row_count // group_rows
    shaped = tuple((member.reshape((blocks, group_rows) + member.shape[1:]) for member in arrays))
    results = lax.map(lambda pieces: kernel(*pieces), shaped)
    return jax.tree.map(lambda member: member.reshape((row_count,) + member.shape[2:]), results)


def attend_block(queries, key_rows, value_rows, allowed):
    scores = jnp.einsum("rqhd,rkhd->rhqk", queries, key_rows, preferred_element_type=jnp.float32)
    scores = jnp.where(allowed[:, None], scores, NEG_FILL)
    peak_score = jnp.max(scores, -1, keepdims=True)
    weights = jnp.exp(scores - peak_score)
    totals = jnp.sum(weights, -1, keepdims=True)
    prob_low = (weights / totals).astype(jnp.bfloat16)
    output = jnp.einsum("rhqk,rkhd->rqhd", prob_low, value_rows, preferred_element_type=jnp.float32)
    return (output, (peak_score + jnp.log(totals))[..., 0])


def attend_back(queries, key_rows, value_rows, allowed, log_total, grad_rows):
    scores = jnp.einsum("rqhd,rkhd->rhqk", queries, key_rows, preferred_element_type=jnp.float32)
    scores = jnp.where(allowed[:, None], scores, NEG_FILL)
    prob_full = jnp.exp(scores - log_total[..., None])
    prob_low = prob_full.astype(jnp.bfloat16)
    value_grad = jnp.einsum(
        "rhqk,rqhd->rkhd", prob_low, grad_rows, preferred_element_type=jnp.float32
    )
    prob_grad = jnp.einsum(
        "rqhd,rkhd->rhqk", grad_rows, value_rows, preferred_element_type=jnp.float32
    )
    offset = jnp.sum(prob_full * prob_grad, -1, keepdims=True)
    score_grad = (prob_full * (prob_grad - offset)).astype(jnp.bfloat16)
    query_grad = jnp.einsum(
        "rhqk,rkhd->rqhd", score_grad, key_rows, preferred_element_type=jnp.float32
    )
    key_grad = jnp.einsum(
        "rhqk,rqhd->rkhd", score_grad, queries, preferred_element_type=jnp.float32
    )
    return (query_grad, key_grad, value_grad)


def body(
    hidden,
    memory,
    out_grad,
    dec_starts,
    dec_length,
    mem_starts,
    mem_length,
    self_qkv,
    self_qv_bias,
    self_proj,
    cross_query,
    cross_kv,
    cross_qv_bias,
    cross_proj,
    ffn_in,
    ffn_in_bias,
    ffn_out,
    out_biases,
    norm_gains,
    norm_biases,
):
    row_count = dec_starts.shape[0]
    dec_slots = hidden.shape[0] // row_count
    mem_slots = memory.shape[0] // row_count
    local_width = self_qkv.shape[2]
    head_count = local_width // HD
    scaling = HD ** (-0.5)
    dec_places = jnp.arange(dec_slots, dtype=jnp.int32)
    mem_places = jnp.arange(mem_slots, dtype=jnp.int32)
    dec_segment = segment_ids(dec_starts, dec_slots)
    mem_segment = segment_ids(mem_starts, mem_slots)
    self_allowed = (
        (dec_segment[:, :, None] == dec_segment[:, None, :])
        & (dec_places[None, None, :] <= dec_places[None, :, None])
        & (dec_places[None, None, :] < dec_length[:, None, None])
    )
    cross_allowed = (dec_segment[:, :, None] == mem_segment[:, None, :]) & (
        mem_places[None, None, :] < mem_length[:, None, None]
    )

    def split_heads(values):
        return values.reshape(row_count, values.shape[0] // row_count, head_count, HD)

    def merge_heads(values):
        return values.reshape(row_count * values.shape[1], local_width)

    self_weight = jnp.concatenate([self_qkv[0], self_qkv[1], self_qkv[2]], axis=1)
    projected = jnp.dot(hidden, self_weight, preferred_element_type=jnp.float32)
    self_q = split_heads(
        ((projected[:, :local_width] + self_qv_bias[0]) * scaling).astype(jnp.bfloat16)
    )
    self_k = split_heads(projected[:, local_width : 2 * local_width].astype(jnp.bfloat16))
    self_v = split_heads((projected[:, 2 * local_width :] + self_qv_bias[1]).astype(jnp.bfloat16))
    self_out, self_total = row_groups(attend_block, (self_q, self_k, self_v, self_allowed))
    self_low = merge_heads(self_out).astype(jnp.bfloat16)
    self_branch = lax.psum(jnp.dot(self_low, self_proj, preferred_element_type=jnp.float32), "mp")
    first, first_back = jax.vjp(
        layer_norm,
        hidden.astype(jnp.float32) + self_branch + out_biases[0],
        norm_gains[0],
        norm_biases[0],
    )
    first_low = first.astype(jnp.bfloat16)
    cross_pre = jnp.dot(first_low, cross_query, preferred_element_type=jnp.float32)
    cross_q = split_heads(((cross_pre + cross_qv_bias[0]) * scaling).astype(jnp.bfloat16))
    memory_whole = lax.all_gather(memory, "mp", axis=1, tiled=True)
    kv_weight = jnp.concatenate([cross_kv[0], cross_kv[1]], axis=1)
    memory_kv = jnp.dot(memory_whole, kv_weight, preferred_element_type=jnp.float32)
    cross_k = split_heads(memory_kv[:, :local_width].astype(jnp.bfloat16))
    cross_v = split_heads((memory_kv[:, local_width:] + cross_qv_bias[1]).astype(jnp.bfloat16))
    cross_out, cross_total = row_groups(attend_block, (cross_q, cross_k, cross_v, cross_allowed))
    cross_low = merge_heads(cross_out).astype(jnp.bfloat16)
    cross_branch = lax.psum(
        jnp.dot(cross_low, cross_proj, preferred_element_type=jnp.float32), "mp"
    )
    second, second_back = jax.vjp(
        layer_norm, first + cross_branch + out_biases[1], norm_gains[1], norm_biases[1]
    )
    second_low = second.astype(jnp.bfloat16)
    hidden_pre = jnp.dot(second_low, ffn_in, preferred_element_type=jnp.float32) + ffn_in_bias
    activated, gelu_back = jax.vjp(exact_gelu, hidden_pre)
    activated_low = activated.astype(jnp.bfloat16)
    ffn_branch = lax.psum(jnp.dot(activated_low, ffn_out, preferred_element_type=jnp.float32), "mp")
    final_norm, third_back = jax.vjp(
        layer_norm, second + ffn_branch + out_biases[2], norm_gains[2], norm_biases[2]
    )
    third_grad, gain_three, shift_three = third_back(out_grad.astype(jnp.float32))
    third_low = third_grad.astype(jnp.bfloat16)
    ffn_out_grad = inner_dot(activated_low, third_low)
    ffn_bias_out = jnp.sum(third_grad, 0)
    (pre_grad,) = gelu_back(outer_dot(third_low, ffn_out))
    ffn_in_bias_grad = jnp.sum(pre_grad, 0)
    pre_low = pre_grad.astype(jnp.bfloat16)
    ffn_in_grad = inner_dot(second_low, pre_low)
    second_grad = third_grad + lax.psum(outer_dot(pre_low, ffn_in), "mp")
    cross_grad, gain_two, shift_two = second_back(second_grad)
    cross_grad_low = cross_grad.astype(jnp.bfloat16)
    cross_proj_grad = inner_dot(cross_low, cross_grad_low)
    cross_bias_out = jnp.sum(cross_grad, 0)
    cross_out_grad = split_heads(outer_dot(cross_grad_low, cross_proj).astype(jnp.bfloat16))
    cq_grad, ck_grad, cv_grad = row_groups(
        attend_back, (cross_q, cross_k, cross_v, cross_allowed, cross_total, cross_out_grad)
    )
    cq_grad = merge_heads(cq_grad) * scaling
    cv_grad = merge_heads(cv_grad)
    cross_qv_grad = jnp.stack([jnp.sum(cq_grad, 0), jnp.sum(cv_grad, 0)])
    cq_low = cq_grad.astype(jnp.bfloat16)
    cross_query_grad = inner_dot(first_low, cq_low)
    first_grad = cross_grad + lax.psum(outer_dot(cq_low, cross_query), "mp")
    kv_grad_low = jnp.concatenate([merge_heads(ck_grad), cv_grad], axis=1).astype(jnp.bfloat16)
    kv_weight_grad = inner_dot(memory_whole, kv_grad_low)
    cross_kv_grad = jnp.stack([kv_weight_grad[:, :local_width], kv_weight_grad[:, local_width:]])
    memory_grad = lax.psum_scatter(
        outer_dot(kv_grad_low, kv_weight).astype(jnp.bfloat16),
        "mp",
        scatter_dimension=1,
        tiled=True,
    ).astype(jnp.float32)
    self_grad, gain_one, shift_one = first_back(first_grad)
    self_grad_low = self_grad.astype(jnp.bfloat16)
    self_proj_grad = inner_dot(self_low, self_grad_low)
    self_bias_out = jnp.sum(self_grad, 0)
    self_out_grad = split_heads(outer_dot(self_grad_low, self_proj).astype(jnp.bfloat16))
    sq_grad, sk_grad, sv_grad = row_groups(
        attend_back, (self_q, self_k, self_v, self_allowed, self_total, self_out_grad)
    )
    sq_grad = merge_heads(sq_grad) * scaling
    sv_grad = merge_heads(sv_grad)
    self_qv_grad = jnp.stack([jnp.sum(sq_grad, 0), jnp.sum(sv_grad, 0)])
    qkv_low = jnp.concatenate([sq_grad, merge_heads(sk_grad), sv_grad], axis=1).astype(jnp.bfloat16)
    qkv_weight_grad = inner_dot(hidden, qkv_low)
    self_qkv_grad = jnp.stack(
        [
            qkv_weight_grad[:, :local_width],
            qkv_weight_grad[:, local_width : 2 * local_width],
            qkv_weight_grad[:, 2 * local_width :],
        ]
    )
    hidden_grad = self_grad + lax.psum(
        outer_dot(qkv_low, self_weight).astype(jnp.bfloat16), "mp"
    ).astype(jnp.float32)
    (
        self_qkv_grad,
        self_qv_grad,
        self_proj_grad,
        cross_query_grad,
        cross_kv_grad,
        cross_qv_grad,
        cross_proj_grad,
        ffn_in_grad,
        ffn_in_bias_grad,
        ffn_out_grad,
        self_bias_out,
        cross_bias_out,
        ffn_bias_out,
        gain_one,
        gain_two,
        gain_three,
        shift_one,
        shift_two,
        shift_three,
    ) = lax.psum(
        (
            self_qkv_grad,
            self_qv_grad,
            self_proj_grad,
            cross_query_grad,
            cross_kv_grad,
            cross_qv_grad,
            cross_proj_grad,
            ffn_in_grad,
            ffn_in_bias_grad,
            ffn_out_grad,
            self_bias_out,
            cross_bias_out,
            ffn_bias_out,
            gain_one,
            gain_two,
            gain_three,
            shift_one,
            shift_two,
            shift_three,
        ),
        "dp",
    )
    out_biases_grad = jnp.stack([self_bias_out, cross_bias_out, ffn_bias_out])
    norm_gains_grad = jnp.stack([gain_one, gain_two, gain_three])
    norm_biases_grad = jnp.stack([shift_one, shift_two, shift_three])
    return (
        final_norm.astype(jnp.bfloat16),
        hidden_grad,
        memory_grad,
        self_qkv_grad,
        self_qv_grad,
        self_proj_grad,
        cross_query_grad,
        cross_kv_grad,
        cross_qv_grad,
        cross_proj_grad,
        ffn_in_grad,
        ffn_in_bias_grad,
        ffn_out_grad,
        out_biases_grad,
        norm_gains_grad,
        norm_biases_grad,
    )


def solution(mesh):
    placed = (
        P("dp", None),
        P("dp", "mp"),
        P("dp", None),
        P("dp", None),
        P("dp"),
        P("dp", None),
        P("dp"),
        P(None, None, "mp"),
        P(None, "mp"),
        P("mp", None),
        P(None, "mp"),
        P(None, None, "mp"),
        P(None, "mp"),
        P("mp", None),
        P(None, "mp"),
        P("mp"),
        P("mp", None),
        P(),
        P(),
        P(),
    )
    return jax.shard_map(
        body,
        mesh=mesh,
        in_specs=placed,
        out_specs=(
            P("dp", None),
            P("dp", None),
            P("dp", "mp"),
            P(None, None, "mp"),
            P(None, "mp"),
            P("mp", None),
            P(None, "mp"),
            P(None, None, "mp"),
            P(None, "mp"),
            P("mp", None),
            P(None, "mp"),
            P("mp"),
            P("mp", None),
            P(),
            P(),
            P(),
        ),
        check_vma=False,
    )
```

profile of v0, /device:TPU:0, one launch (start us, length us, event | category | flops | bytes accessed | tf_op | source)
XLA Modules:
  0.0 875.1 jit_solution(11104530872102401639)
XLA Ops:
  13.4 1.6 fusion.63
  17.6 69.4 %all-reduce.10.cloned.1.call-done = f32[512,768]{1,0:T(8,128)} async-done(((f32[512,768]{1,0:T(8,128)}), f32[512,768]{1,0:T(8,128)}) %all-reduce.10.cloned.1.call-update) | async-done | bytes 1572880 | tf_op jit(solution)/shard_map/psum | solution.py:140
  87.0 1.9 fusion.103
  92.5 110.5 %all-gather.2.cloned.1.call-done = bf16[4096,768]{0,1:T(8,128)(2,1)} async-done(((bf16[4096,192]{0,1:T(8,128)(2,1)}), bf16[4096,768]{0,1:T(8,128)(2,1)}) %all-gather.2.cloned.1.call-update) | async-done | bytes 6291472 | tf_op jit(solution)/shard_map/all_gather | solution.py:150
  203.0 4.8 convolution_bitcast_fusion
  207.8 2.6 copy-done.17
  211.8 3.9 squeeze.90
  215.7 3.4 fusion.4
  219.0 3.9 squeeze.88
  222.9 3.5 select_reduce_fusion
  226.4 1.6 fusion
  229.1 2.8 fusion.39
  232.0 1.6 fusion.59
  233.8 67.3 %all-reduce.12.cloned.1.call-done = f32[512,768]{1,0:T(8,128)} async-done(((f32[512,768]{1,0:T(8,128)}), f32[512,768]{1,0:T(8,128)}) %all-reduce.12.cloned.1.call-update) | async-done | bytes 1572880 | tf_op jit(solution)/shard_map/psum | solution.py:157
  301.1 2.0 fusion.102
  303.8 5.4 multiply_convert_fusion.1
  310.1 1.9 fusion.115
  312.1 68.3 %all-reduce.14.cloned.1.call-done = f32[512,768]{1,0:T(8,128)} async-done(((f32[512,768]{1,0:T(8,128)}), f32[512,768]{1,0:T(8,128)}) %all-reduce.14.cloned.1.call-update) | async-done | bytes 1572880 | tf_op jit(solution)/shard_map/psum | solution.py:167
  380.4 2.0 fusion.100
  384.2 1.6 fusion.99
  386.7 1.8 fusion.110
  389.5 2.0 fusion.51
  391.6 68.2 %all-reduce.16.cloned.1.call-done = f32[512,768]{1,0:T(8,128)} async-done(((f32[512,768]{1,0:T(8,128)}), f32[512,768]{1,0:T(8,128)}) %all-reduce.16.cloned.1.call-update) | async-done | bytes 1572880 | tf_op jit(solution)/shard_map/psum | solution.py:179
  459.8 2.8 multiply_reduce_fusion.1
  465.0 6.5 multiply_reduce_fusion
  471.5 1.8 multiply_convert_fusion
  473.4 2.1 fusion.104
  475.6 1.6 fusion.55
  477.5 2.6 fusion.19
  482.0 3.1 bitcast_convert_fusion
  486.4 1.8 copy.123
  489.5 56.1 %all-reduce.18.cloned.1.call-done = f32[512,768]{1,0:T(8,128)} async-done(((f32[512,768]{1,0:T(8,128)}), f32[512,768]{1,0:T(8,128)}) %all-reduce.18.cloned.1.call-update) | async-done | bytes 1572880 | tf_op jit(solution)/shard_map/psum | solution.py:193
  545.6 2.8 multiply_reduce_fusion.2
  553.6 1.7 convolution_convert_fusion.2
  556.6 7.2 convolution_convert_fusion
  565.0 3.8 fusion.93
  568.8 2.4 fusion.49
  571.2 5.5 convolution_bitcast_fusion.3
  584.9 2.1 bitcast_reduce_fusion
  587.4 10.8 %all-reduce.20.cloned.1.call-done = bf16[512,768]{1,0:T(8,128)(2,1)} async-done(((bf16[512,768]{1,0:T(8,128)(2,1)}), bf16[512,768]{1,0:T(8,128)(2,1)}) %all-reduce.20.cloned.1.call-update) | async-done | bytes 786448 | tf_op jit(solution)/shard_map/psum | solution.py:223
  598.2 2.5 add_reduce_fusion
  600.8 25.6 %all-reduce = (f32[2,192]{1,0:T(2,128)}, f32[2,192]{1,0:T(2,128)}, f32[768]{0:T(1024)}, f32[1,768]{1,0:T(1,128)S(1)}, f32[1,768]{1,0:T(1,128)S(1)}, /*index=5*/f...) all-reduce(f32[2,192]{1,0:T(2,128)S(1)} %pad_maximum_fusion.11, ...), channel_id=1, replica_groups=mesh['dp'=8,'mp'=4] {'dp'}, use_global_device_ids=true, to_apply=%region_30.31 | all-reduce | flops 8448 | bytes 67584 | tf_op jit(solution)/shard_map/psum | solution.py:246
  628.2 82.3 %reduce-scatter.2.cloned.1.call-done = bf16[4096,192]{0,1:T(8,128)(2,1)} async-done(((bf16[4096,768]{0,1:T(8,128)(2,1)}), bf16[4096,192]{0,1:T(8,128)(2,1)}) %reduce-scatter.2.cloned.1.call-update) | async-done | bytes 1572880 | tf_op jit(solution)/shard_map/reduce_scatter | solution.py:197
  710.5 3.4 convert_element_type.157
  714.0 143.3 %all-reduce.22.cloned.1.call-done = (f32[3,768,192]{1,2,0:T(8,128)}, f32[192,768]{1,0:T(8,128)}, f32[768,192]{0,1:T(8,128)}, f32[2,768,192]{1,2,0:T(8,128)}, f32...) async-done(((f32[3,768,192]{1,2,0:T(8,128)}, f32[192,768]{1,0:T(8,128)}, f32[768,192]{0,1:T(8,128)}, f32[2,768,192]{1,2,0:T(8,128)}, f32[192,768]{1,0:T(8,128)}, ...) | async-done | bytes 9437200 | tf_op jit(solution)/shard_map/psum | solution.py:246
  857.3 2.9 copy.229
  864.2 1.4 copy.234
  866.7 1.4 copy.235
  (292 shorter events, 50.4 us)
Async XLA Ops:
  7.2 296.3 %copy-start = (bf16[768,768]{1,0:T(8,128)(2,1)S(1)}, bf16[768,768]{1,0:T(8,128)(2,1)}, u32[]{:S(2)}) copy-start(bf16[768,768]{1,0:T(8,128)(2,1)} %param.34) | copy-start | bytes 3538948
  7.2 2.2 copy-start.25
  7.2 79.8 %all-reduce.10.cloned.1.call-start = ((), (), s32[]{:S(2)}) async-start(), calls=%async_computation.1 | async-start | bytes 3145728 | tf_op jit(solution)/shard_map/psum | solution.py:140
  15.0 188.0 %all-gather.2.cloned.1.call-start = ((), (), s32[]{:S(2)}) async-start(), calls=%async_computation.2 | async-start | bytes 7864320 | tf_op jit(solution)/shard_map/all_gather | solution.py:150
  15.8 285.3 %all-reduce.12.cloned.1.call-start = ((), (), s32[]{:S(2)}) async-start(), calls=%async_computation.3 | async-start | bytes 3145728 | tf_op jit(solution)/shard_map/psum | solution.py:157
  16.1 364.2 %copy-start.63 = (f32[768]{0:T(1024)}, f32[768]{0:T(1024)S(1)}, u32[]{:S(2)}) copy-start(f32[768]{0:T(1024)S(1)} %get-tuple-element.122) | copy-start | bytes 9220
  16.7 211.4 %copy-start.12 = (pred[4,128,1024]{2,1,0:T(8,128)(4,1)}, pred[4,128,1024]{2,1,0:T(8,128)(4,1)S(1)}, u32[]{:S(2)}) copy-start(pred[4,128,1024]{2,1,0:T(8,128)(4,1)S(1)} %compare_and_fusion) | copy-start | bytes 1572868
  88.9 212.2 %copy-start.3 = (f32[512,768]{1,0:T(8,128)}, f32[512,768]{1,0:T(8,128)S(1)}, u32[]{:S(2)}) copy-start(f32[512,768]{1,0:T(8,128)S(1)} %get-tuple-element.170) | copy-start | bytes 4718596
  207.8 2.7 copy-start.17
  226.4 2.7 copy-start.2
  226.4 2.7 copy-start.21
  229.1 2.9 copy-start.39
  233.6 146.7 %all-reduce.14.cloned.1.call-start = ((), (), s32[]{:S(2)}) async-start(), calls=%async_computation.4 | async-start | bytes 3145728 | tf_op jit(solution)/shard_map/psum | solution.py:167
  303.1 6.1 copy-start.5
  303.8 6.3 copy-start.74
  312.0 68.3 %copy-start.6 = (f32[512,768]{1,0:T(8,128)S(1)}, f32[512,768]{1,0:T(8,128)}, u32[]{:S(2)}) copy-start(f32[512,768]{1,0:T(8,128)} %copy-done.5) | copy-start | bytes 4718596
  312.0 147.8 %all-reduce.16.cloned.1.call-start = ((), (), s32[]{:S(2)}) async-start(), calls=%async_computation.5 | async-start | bytes 3145728 | tf_op jit(solution)/shard_map/psum | solution.py:179
  384.2 1.9 copy-start.80
  384.2 2.5 copy-start.81
  385.8 2.7 copy-start.18
  391.5 154.1 %all-reduce.18.cloned.1.call-start = ((), (), s32[]{:S(2)}) async-start(), calls=%async_computation.6 | async-start | bytes 3145728 | tf_op jit(solution)/shard_map/psum | solution.py:193
  462.6 1.8 copy-start.40
  465.0 6.5 slice-start
  465.0 6.5 slice-start.1
  473.3 2.1 copy-start.14
  473.3 2.3 copy-start.62
  477.2 4.8 slice-start.2
  477.2 121.0 %all-reduce.20.cloned.1.call-start = ((), (), s32[]{:S(2)}) async-start(), calls=%async_computation.7 | async-start | bytes 1572864 | tf_op jit(solution)/shard_map/psum | solution.py:223
  477.5 4.5 slice-start.3
  488.2 57.4 %copy-start.4 = (f32[512,768]{1,0:T(8,128)S(1)}, f32[512,768]{1,0:T(8,128)}, u32[]{:S(2)}) copy-start(f32[512,768]{1,0:T(8,128)} %copy-done.3) | copy-start | bytes 4718596
  555.3 155.2 %reduce-scatter.2.cloned.1.call-start = ((), (), s32[]{:S(2)}) async-start(), calls=%async_computation.8 | async-start | bytes 7864320 | tf_op jit(solution)/shard_map/reduce_scatter | solution.py:197
  563.9 4.9 copy-start.7
  563.9 4.9 copy-start.64
  563.9 293.4 %all-reduce.22.cloned.1.call-start = ((), (), s32[]{:S(2)}) async-start(), calls=%async_computation.9 | async-start | bytes 18874368 | tf_op jit(solution)/shard_map/psum | solution.py:246
  565.0 3.8 copy-start.79
  568.8 2.4 copy-start.46
  576.8 2.7 copy-start.11
  576.8 2.7 copy-start.38
  581.4 2.1 copy-start.9
  581.5 2.1 copy-start.36
  584.8 2.2 copy-start.70
  587.4 13.4 %copy-start.68 = (f32[768]{0:T(1024)S(1)}, f32[768]{0:T(1024)}, u32[]{:S(2)}) copy-start(f32[768]{0:T(1024)} %get-tuple-element.210) | copy-start | bytes 9220
  857.3 2.9 copy-start.54
  857.3 3.7 copy-start.53
  861.0 1.8 copy-start.52
  861.8 2.3 copy-start.28
  864.2 2.5 copy-start.27
  864.2 3.9 copy-start.1
  (47 other events, 56.8 us)
Sparse Core Ops, SparseCore 0:
  15.2 71.7 all-reduce.9
  88.6 114.3 all-gather.1
  233.7 67.3 all-reduce.11
  312.2 68.1 all-reduce.13
  391.6 68.1 all-reduce.15
  477.4 68.1 all-reduce.17
  555.4 42.7 all-reduce.19
  600.5 109.9 reduce-scatter.1
  716.5 140.7 all-reduce.21
where the time goes:
time: 884 us; the launch traced here: 875 us
  waiting for transfers between devices  677 us (77%)
  matrix products  70.8 us (8%)
  local copies, waits for them, and re-layouts  47.4 us (5%)
  other arithmetic  37.7 us (4%)
  blocking collectives  25.6 us (3%)
  between operations  15.5 us (2%)
    psum x1, waiting for transfers between devices, body(): lax.psum((self_qkv_grad, self_qv_grad, self_proj_grad, cross_query_grad,...  143 us
    all_gather x1, waiting for transfers between devices, body(): memory_whole = lax.all_gather(memory, 'mp', axis=1, tiled=True)  110 us
    reduce_scatter x1, waiting for transfers between devices, body(): lax.psum_scatter(outer_dot(kv_grad_low, kv_weight).astype(jnp.bfloat16),...  82.3 us
    psum x1, waiting for transfers between devices, body(): lax.psum(jnp.dot(self_low, self_proj, preferred_element_type=jnp.float32)...  69.4 us
    psum x1, waiting for transfers between devices, body(): lax.psum(jnp.dot(activated_low, ffn_out, preferred_element_type=jnp.float...  68.3 us
    psum x1, waiting for transfers between devices, body(): second_grad = third_grad + lax.psum(outer_dot(pre_low, ffn_in), 'mp')  68.2 us
    psum x1, waiting for transfers between devices, body(): lax.psum(jnp.dot(cross_low, cross_proj, preferred_element_type=jnp.float3...  67.3 us
    psum x1, waiting for transfers between devices, body(): first_grad = cross_grad + lax.psum(outer_dot(cq_low, cross_query), 'mp')  56.1 us
  transfers between devices with their start and end apart: 9, of which 9 were waited for; matrix products, arithmetic and copies ran while one was open for 6% of the time, Pallas kernels for 0%

commit v1 on v0

--- a/solution.py
+++ b/solution.py
@@ -147,7 +147,23 @@
     first_low = first.astype(jnp.bfloat16)
     cross_pre = jnp.dot(first_low, cross_query, preferred_element_type=jnp.float32)
     cross_q = split_heads(((cross_pre + cross_qv_bias[0]) * scaling).astype(jnp.bfloat16))
-    memory_whole = lax.all_gather(memory, "mp", axis=1, tiled=True)
+    side_arr, newest, g_now = (lax.axis_size("mp"), lax.axis_index("mp"), memory.shape[1])
+    grid = tuple(((hop_no, (hop_no + 1) % side_arr) for hop_no in range(side_arr)))
+    table = tuple(((hop_no, (hop_no - 1) % side_arr) for hop_no in range(side_arr)))
+    memory_whole = jnp.zeros((*memory.shape[:1], side_arr * g_now, *memory.shape[2:]), memory.dtype)
+    kept_arr = x_now = memory
+    q_next = side_arr // 2
+    memory_whole = lax.dynamic_update_slice_in_dim(memory_whole, memory, newest * g_now, axis=1)
+    for to_i in range(1, q_next + 1):
+        kept_arr = lax.ppermute(kept_arr, axis_name="mp", perm=grid)
+        memory_whole = lax.dynamic_update_slice_in_dim(
+            memory_whole, kept_arr, (newest - to_i) % side_arr * g_now, axis=1
+        )
+        if to_i < side_arr - q_next:
+            x_now = lax.ppermute(x_now, axis_name="mp", perm=table)
+            memory_whole = lax.dynamic_update_slice_in_dim(
+                memory_whole, x_now, (newest + to_i) % side_arr * g_now, axis=1
+            )
     kv_weight = jnp.concatenate([cross_kv[0], cross_kv[1]], axis=1)
     memory_kv = jnp.dot(memory_whole, kv_weight, preferred_element_type=jnp.float32)
     cross_k = split_heads(memory_kv[:, :local_width].astype(jnp.bfloat16))

time: 884 us -> 855 us (0.967)
  waiting for transfers between devices: 677 us -> 595 us
  starting transfers between devices: 1.01 us -> 45.1 us
  local copies, waits for them, and re-layouts: 47.4 us -> 60.3 us
    all_gather x1 -> x0, waiting for transfers between devices: 110 us -> none  [body(): memory_whole = lax.all_gather(memory, 'mp', axis=1, tiled=True)]
    ppermute x0 -> x3, starting transfers between devices: none -> 44.1 us  [the longest x2 42 us: body(): kept_arr = lax.ppermute(kept_arr, axis_name='mp', perm=grid)]
    ppermute x0 -> x3, waiting for transfers between devices: none -> 39.8 us  [the longest x2 39.8 us: body(): kept_arr = lax.ppermute(kept_arr, axis_name='mp', perm=grid)]
    psum x1, waiting for transfers between devices: 69.4 us -> 58.7 us  [body(): lax.psum(jnp.dot(self_low, self_proj, preferred_element_type=jnp.float32)...]
    dynamic_update_slice x0 -> x4, local copies, waits for them, and re-layouts: none -> 9.47 us  [the longest x2 5.51 us: body(): lax.dynamic_update_slice_in_dim(memory_whole, kept_arr, (newest - to_i) %...]
    unnamed x184 -> x190, local copies, waits for them, and re-layouts: 29.7 us -> 29.6 us
  transfers between devices with their start and end apart: 9 -> 11, of which waited for: 9 -> 9; matrix products, arithmetic and copies ran while one was open for 6% -> 8% of each run, Pallas kernels for 0% -> 0%
where the time goes in v1:
time: 855 us; the launch traced here: 850 us
  waiting for transfers between devices  595 us (70%)
  matrix products  71 us (8%)
  local copies, waits for them, and re-layouts  60.3 us (7%)
  starting transfers between devices  45.1 us (5%)
  other arithmetic  37.6 us (4%)
  blocking collectives  25.6 us (3%)
  between operations  15.6 us (2%)
    psum x1, waiting for transfers between devices, body(): lax.psum((self_qkv_grad, self_qv_grad, self_proj_grad, cross_query_grad,...  143 us
    reduce_scatter x1, waiting for transfers between devices, body(): lax.psum_scatter(outer_dot(kv_grad_low, kv_weight).astype(jnp.bfloat16),...  82.4 us
    psum x1, waiting for transfers between devices, body(): second_grad = third_grad + lax.psum(outer_dot(pre_low, ffn_in), 'mp')  68.2 us
    psum x1, waiting for transfers between devices, body(): lax.psum(jnp.dot(activated_low, ffn_out, preferred_element_type=jnp.float...  68.1 us
    psum x1, waiting for transfers between devices, body(): lax.psum(jnp.dot(cross_low, cross_proj, preferred_element_type=jnp.float3...  67.5 us
    psum x1, waiting for transfers between devices, body(): lax.psum(jnp.dot(self_low, self_proj, preferred_element_type=jnp.float32)...  58.7 us
    psum x1, waiting for transfers between devices, body(): first_grad = cross_grad + lax.psum(outer_dot(cq_low, cross_query), 'mp')  56.1 us
    ppermute x2, starting transfers between devices, body(): kept_arr = lax.ppermute(kept_arr, axis_name='mp', perm=grid)  42 us
  transfers between devices with their start and end apart: 11, of which 9 were waited for; matrix products, arithmetic and copies ran while one was open for 8% of the time, Pallas kernels for 0%

profile of v1, /device:TPU:0, one launch (start us, length us, event | category | flops | bytes accessed | tf_op | source)
XLA Modules:
  0.0 850.0 jit_solution(8673292777087268438)
XLA Ops:
  7.3 3.1 collective-permute-start
  10.3 2.1 collective-permute-start.1
  22.0 3.4 broadcast_in_dim.139
  26.7 39.8 %collective-permute-done = bf16[4096,192]{0,1:T(8,128)(2,1)} collective-permute-done((bf16[4096,192]{0,1:T(8,128)(2,1)}, bf16[4096,192]{0,1:T(8,128)(2,1)}, u32[]{:S(2)}, u32[]{:S(2)}) %collective-permute-start) | collective-permute-done | bytes 1572896 | tf_op jit(solution)/shard_map/ppermute | solution.py:158
  66.6 39.0 %collective-permute-start.2 = (bf16[4096,192]{0,1:T(8,128)(2,1)}, bf16[4096,192]{0,1:T(8,128)(2,1)}, u32[]{:S(2)}, u32[]{:S(2)}) collective-permute-start(bf16[4096,192]{0,1:T(8,128)(2,1)} %collective-permute-done), channel_id=1, source_target_pairs={{0,1},{1,2},{2,3},{3,0},{4,5},{5,6},{6,7},{7,4},{8,9},{9,10},{10,1... | collective-permute-start | bytes 4718600 | tf_op jit(solution)/shard_map/ppermute | solution.py:158
  105.5 58.7 %all-reduce.10.cloned.1.call-done = f32[512,768]{1,0:T(8,128)} async-done(((f32[512,768]{1,0:T(8,128)}), f32[512,768]{1,0:T(8,128)}) %all-reduce.10.cloned.1.call-update) | async-done | bytes 1572880 | tf_op jit(solution)/shard_map/psum | solution.py:140
  164.2 1.9 fusion.104
  169.7 2.7 constant_dynamic-update-slice_fusion.4
  172.4 2.7 constant_dynamic-update-slice_fusion.3
  175.2 2.8 constant_dynamic-update-slice_fusion.2
  177.9 4.7 fusion.53
  182.7 2.6 copy-done.17
  186.6 3.9 squeeze.90
  190.5 3.4 fusion.4
  193.8 3.9 squeeze.88
  197.7 3.5 select_reduce_fusion
  203.9 2.8 fusion.39
  208.5 67.5 %all-reduce.12.cloned.1.call-done = f32[512,768]{1,0:T(8,128)} async-done(((f32[512,768]{1,0:T(8,128)}), f32[512,768]{1,0:T(8,128)}) %all-reduce.12.cloned.1.call-update) | async-done | bytes 1572880 | tf_op jit(solution)/shard_map/psum | solution.py:173
  276.0 2.0 fusion.103
  278.7 5.4 multiply_convert_fusion.1
  285.0 1.9 fusion.116
  287.1 68.1 %all-reduce.14.cloned.1.call-done = f32[512,768]{1,0:T(8,128)} async-done(((f32[512,768]{1,0:T(8,128)}), f32[512,768]{1,0:T(8,128)}) %all-reduce.14.cloned.1.call-update) | async-done | bytes 1572880 | tf_op jit(solution)/shard_map/psum | solution.py:183
  355.2 2.0 fusion.101
  361.6 1.8 fusion.111
  364.3 2.0 fusion.51
  366.4 68.2 %all-reduce.16.cloned.1.call-done = f32[512,768]{1,0:T(8,128)} async-done(((f32[512,768]{1,0:T(8,128)}), f32[512,768]{1,0:T(8,128)}) %all-reduce.16.cloned.1.call-update) | async-done | bytes 1572880 | tf_op jit(solution)/shard_map/psum | solution.py:195
  434.6 2.8 multiply_reduce_fusion.1
  439.8 6.5 multiply_reduce_fusion
  446.3 1.8 multiply_convert_fusion
  448.1 2.1 fusion.105
  452.3 2.6 fusion.19
  456.8 3.2 bitcast_convert_fusion
  461.2 1.8 copy.123
  464.2 56.1 %all-reduce.18.cloned.1.call-done = f32[512,768]{1,0:T(8,128)} async-done(((f32[512,768]{1,0:T(8,128)}), f32[512,768]{1,0:T(8,128)}) %all-reduce.18.cloned.1.call-update) | async-done | bytes 1572880 | tf_op jit(solution)/shard_map/psum | solution.py:209
  520.3 2.8 multiply_reduce_fusion.2
  528.3 1.7 convolution_convert_fusion.2
  531.4 7.2 convolution_convert_fusion
  539.8 3.8 fusion.94
  543.6 2.4 fusion.49
  546.0 5.6 fusion.117
  559.8 2.1 bitcast_reduce_fusion
  562.4 10.5 %all-reduce.20.cloned.1.call-done = bf16[512,768]{1,0:T(8,128)(2,1)} async-done(((bf16[512,768]{1,0:T(8,128)(2,1)}), bf16[512,768]{1,0:T(8,128)(2,1)}) %all-reduce.20.cloned.1.call-update) | async-done | bytes 786448 | tf_op jit(solution)/shard_map/psum | solution.py:239
  572.9 2.5 add_reduce_fusion
  575.5 25.6 %all-reduce = (f32[2,192]{1,0:T(2,128)}, f32[2,192]{1,0:T(2,128)}, f32[768]{0:T(1024)}, f32[1,768]{1,0:T(1,128)S(1)}, f32[1,768]{1,0:T(1,128)S(1)}, /*index=5*/f...) all-reduce(f32[2,192]{1,0:T(2,128)S(1)} %pad_maximum_fusion.11, ...), channel_id=1, replica_groups=mesh['dp'=8,'mp'=4] {'dp'}, use_global_device_ids=true, to_apply=%region_30.31 | all-reduce | flops 8448 | bytes 67584 | tf_op jit(solution)/shard_map/psum | solution.py:262
  602.9 82.4 %reduce-scatter.2.cloned.1.call-done = bf16[4096,192]{0,1:T(8,128)(2,1)} async-done(((bf16[4096,768]{0,1:T(8,128)(2,1)}), bf16[4096,192]{0,1:T(8,128)(2,1)}) %reduce-scatter.2.cloned.1.call-update) | async-done | bytes 1572880 | tf_op jit(solution)/shard_map/reduce_scatter | solution.py:213
  685.3 3.4 convert_element_type.157
  688.7 143.3 %all-reduce.22.cloned.1.call-done = (f32[3,768,192]{1,2,0:T(8,128)}, f32[192,768]{1,0:T(8,128)}, f32[768,192]{0,1:T(8,128)}, f32[2,768,192]{1,2,0:T(8,128)}, f32...) async-done(((f32[3,768,192]{1,2,0:T(8,128)}, f32[192,768]{1,0:T(8,128)}, f32[768,192]{0,1:T(8,128)}, f32[2,768,192]{1,2,0:T(8,128)}, f32[192,768]{1,0:T(8,128)}, ...) | async-done | bytes 9437200 | tf_op jit(solution)/shard_map/psum | solution.py:262
  832.1 2.9 copy.233
  (306 shorter events, 61.5 us)
Async XLA Ops:
  7.2 271.1 %copy-start = (bf16[768,768]{1,0:T(8,128)(2,1)S(1)}, bf16[768,768]{1,0:T(8,128)(2,1)}, u32[]{:S(2)}) copy-start(bf16[768,768]{1,0:T(8,128)(2,1)} %param.34) | copy-start | bytes 3538948
  7.2 7.3 copy-start.25
  7.2 157.0 %all-reduce.10.cloned.1.call-start = ((), (), s32[]{:S(2)}) async-start(), calls=%async_computation.1 | async-start | bytes 3145728 | tf_op jit(solution)/shard_map/psum | solution.py:140
  7.3 59.3 %collective-permute-start = (bf16[4096,192]{0,1:T(8,128)(2,1)}, bf16[4096,192]{0,1:T(8,128)(2,1)}, u32[]{:S(2)}, u32[]{:S(2)}) collective-permute-start(bf16[4096,192]{0,1:T(8,128)(2,1)} %param.21), channel_id=1, source_target_pairs={{0,1},{1,2},{2,3},{3,0},{4,5},{5,6},{6,7},{7,4},{8,9},{9,10},{10,1... | collective-permute-start | bytes 4718600 | tf_op jit(solution)/shard_map/ppermute | solution.py:158
  10.3 162.1 %collective-permute-start.1 = (bf16[4096,192]{0,1:T(8,128)(2,1)}, bf16[4096,192]{0,1:T(8,128)(2,1)}, u32[]{:S(2)}, u32[]{:S(2)}) collective-permute-start(bf16[4096,192]{0,1:T(8,128)(2,1)} %param.21), channel_id=1, source_target_pairs={{0,3},{1,0},{2,1},{3,2},{4,7},{5,4},{6,5},{7,6},{8,11},{9,8},{10,9... | collective-permute-start | bytes 4718600 | tf_op jit(solution)/shard_map/ppermute | solution.py:163
  20.1 255.9 %all-reduce.12.cloned.1.call-start = ((), (), s32[]{:S(2)}) async-start(), calls=%async_computation.2 | async-start | bytes 3145728 | tf_op jit(solution)/shard_map/psum | solution.py:173
  20.5 334.8 %copy-start.66 = (f32[768]{0:T(1024)}, f32[768]{0:T(1024)S(1)}, u32[]{:S(2)}) copy-start(f32[768]{0:T(1024)S(1)} %get-tuple-element.122) | copy-start | bytes 9220
  21.1 181.8 %copy-start.12 = (pred[4,128,1024]{2,1,0:T(8,128)(4,1)}, pred[4,128,1024]{2,1,0:T(8,128)(4,1)S(1)}, u32[]{:S(2)}) copy-start(pred[4,128,1024]{2,1,0:T(8,128)(4,1)S(1)} %compare_and_fusion) | copy-start | bytes 1572868
  22.0 3.4 copy-start.39
  66.6 108.6 %collective-permute-start.2 = (bf16[4096,192]{0,1:T(8,128)(2,1)}, bf16[4096,192]{0,1:T(8,128)(2,1)}, u32[]{:S(2)}, u32[]{:S(2)}) collective-permute-start(bf16[4096,192]{0,1:T(8,128)(2,1)} %collective-permute-done), channel_id=1, source_target_pairs={{0,1},{1,2},{2,3},{3,0},{4,5},{5,6},{6,7},{7,4},{8,9},{9,10},{10,1... | collective-permute-start | bytes 4718600 | tf_op jit(solution)/shard_map/ppermute | solution.py:158
  166.1 109.9 %copy-start.3 = (f32[512,768]{1,0:T(8,128)}, f32[512,768]{1,0:T(8,128)S(1)}, u32[]{:S(2)}) copy-start(f32[512,768]{1,0:T(8,128)S(1)} %get-tuple-element.170) | copy-start | bytes 4718596
  175.2 2.8 copy-start.44
  175.2 2.8 copy-start.46
  182.7 2.6 copy-start.17
  201.2 2.7 copy-start.2
  201.2 2.7 copy-start.21
  203.9 2.9 copy-start.40
  208.4 146.8 %all-reduce.14.cloned.1.call-start = ((), (), s32[]{:S(2)}) async-start(), calls=%async_computation.3 | async-start | bytes 3145728 | tf_op jit(solution)/shard_map/psum | solution.py:183
  278.0 6.1 copy-start.5
  278.7 6.3 copy-start.77
  286.9 68.3 %copy-start.6 = (f32[512,768]{1,0:T(8,128)S(1)}, f32[512,768]{1,0:T(8,128)}, u32[]{:S(2)}) copy-start(f32[512,768]{1,0:T(8,128)} %copy-done.5) | copy-start | bytes 4718596
  286.9 147.7 %all-reduce.16.cloned.1.call-start = ((), (), s32[]{:S(2)}) async-start(), calls=%async_computation.4 | async-start | bytes 3145728 | tf_op jit(solution)/shard_map/psum | solution.py:195
  359.1 2.5 copy-start.84
  360.7 2.7 copy-start.18
  366.3 154.0 %all-reduce.18.cloned.1.call-start = ((), (), s32[]{:S(2)}) async-start(), calls=%async_computation.5 | async-start | bytes 3145728 | tf_op jit(solution)/shard_map/psum | solution.py:209
  439.7 6.5 slice-start
  439.8 6.5 slice-start.1
  448.1 2.1 copy-start.14
  448.1 2.3 copy-start.65
  452.0 4.8 slice-start.2
  452.0 120.9 %all-reduce.20.cloned.1.call-start = ((), (), s32[]{:S(2)}) async-start(), calls=%async_computation.6 | async-start | bytes 1572864 | tf_op jit(solution)/shard_map/psum | solution.py:239
  452.3 4.5 slice-start.3
  462.9 57.4 %copy-start.4 = (f32[512,768]{1,0:T(8,128)S(1)}, f32[512,768]{1,0:T(8,128)}, u32[]{:S(2)}) copy-start(f32[512,768]{1,0:T(8,128)} %copy-done.3) | copy-start | bytes 4718596
  530.1 155.3 %reduce-scatter.2.cloned.1.call-start = ((), (), s32[]{:S(2)}) async-start(), calls=%async_computation.7 | async-start | bytes 7864320 | tf_op jit(solution)/shard_map/reduce_scatter | solution.py:213
  538.7 4.9 copy-start.7
  538.7 4.9 copy-start.67
  538.7 293.4 %all-reduce.22.cloned.1.call-start = ((), (), s32[]{:S(2)}) async-start(), calls=%async_computation.8 | async-start | bytes 18874368 | tf_op jit(solution)/shard_map/psum | solution.py:262
  539.8 3.8 copy-start.82
  543.6 2.4 copy-start.49
  551.7 2.7 copy-start.11
  551.8 2.7 copy-start.38
  559.8 2.2 copy-start.73
  562.4 13.1 %copy-start.71 = (f32[768]{0:T(1024)S(1)}, f32[768]{0:T(1024)}, u32[]{:S(2)}) copy-start(f32[768]{0:T(1024)} %get-tuple-element.210) | copy-start | bytes 9220
  832.1 2.9 copy-start.57
  832.1 3.7 copy-start.56
  836.6 2.3 copy-start.28
  839.0 2.5 copy-start.27
  839.0 3.9 copy-start.1
  (52 other events, 70.8 us)
Sparse Core Ops, SparseCore 0:
  20.2 143.9 all-reduce.9
  208.5 67.3 all-reduce.11
  287.0 68.1 all-reduce.13
  366.5 68.1 all-reduce.15
  452.1 68.1 all-reduce.17
  530.2 42.6 all-reduce.19
  575.2 110.0 reduce-scatter.1
  691.2 140.7 all-reduce.21
